TPU v7x, 256 devices: a whole 4x4x8 slice. The times are simulated.
256 devices in a mesh: seq: 32 (over x_lo, z, core), wt: 8 (over y, x_hi).
Axes of the slice: x: 4 (x_hi: 2, x_lo: 2; x = x_hi * 2 + x_lo), y: 4, z: 8, core: 2. Of those that a mesh axis runs over, the one named last changes fastest.
Arguments:
- tokens: int32 [8, 4096], P('wt', 'seq'), may hold values from 0 to 511
- embed_table: bfloat16 [512, 8192], P(None, 'wt'), may hold values from -8 to 8
- norm_gain: bfloat16 [8192], P('wt'), may hold values from 0.099609375 to 1.8984375
- w_in: bfloat16 [8192, 3, 4096], P('wt', None, 'seq'), may hold values from -0.0625 to 0.0625
- short_taps: bfloat16 [3, 3, 4096], P(None, None, 'seq'), may hold values from -3 to 3
- filters: bfloat16 [256, 128], P('seq'), may hold values from -2 to 2
- w_out: bfloat16 [8192, 4096], P('wt'), may hold values from -0.09375 to 0.09375
Outputs:
- block_out: bfloat16 [8, 4096, 8192], P(None, 'seq', 'wt')
All inputs are finite; a program needn't handle non-finite values.
Results may differ from a plain program's by a relative error of at most 0.0088.
Values may be sent and summed in bfloat16 or wider, within the bound.
A program may use at most 128 MiB of HBM per device.

v0:
```python
import jax
import jax.numpy as jnp
from jax import lax
from jax.sharding import PartitionSpec as P


def shifted(shard, axis, by):
    size = lax.axis_size(axis)
    pairs = [(i, i + by) for i in range(size) if 0 <= i + by < size]
    return lax.ppermute(shard, axis, pairs)


def causal_pair(filter_vals):
    tap_count = filter_vals.shape[1]
    group_count = filter_vals.shape[0]
    tiled_taps = jnp.tile(filter_vals, (1, 2 * tap_count - 1)).reshape(
        group_count, tap_count, 2 * tap_count - 1
    )[:, :, :tap_count]
    circulant = jnp.swapaxes(tiled_taps, 1, 2)
    row_pos = lax.broadcasted_iota(jnp.int32, (tap_count, tap_count), 0)
    col_pos = lax.broadcasted_iota(jnp.int32, (tap_count, tap_count), 1)
    lower_mask = (row_pos >= col_pos)[None]
    zero_mat = jnp.zeros_like(circulant)
    return (jnp.where(lower_mask, circulant, zero_mat), jnp.where(lower_mask, zero_mat, circulant))


def short_mix(extended, tap_vals):
    row_count = extended.shape[0] - 2
    ext_vals = extended.astype(jnp.float32)
    return (
        tap_vals[0] * ext_vals[2 : 2 + row_count]
        + tap_vals[1] * ext_vals[1 : 1 + row_count]
        + tap_vals[2] * ext_vals[0:row_count]
    )


def run_filter(extended, lower_mat, upper_mat):
    tap_count = lower_mat.shape[1]
    group_count = lower_mat.shape[0]
    chan_count = extended.shape[1]
    blocks = extended.shape[0] // tap_count
    stacked = extended.reshape(blocks, tap_count, group_count, chan_count // group_count)
    filtered = jnp.einsum(
        "gij,bjgc->bigc", lower_mat, stacked[1:], preferred_element_type=jnp.float32
    )
    filtered = filtered + jnp.einsum(
        "gij,bjgc->bigc", upper_mat, stacked[:-1], preferred_element_type=jnp.float32
    )
    return filtered.reshape((blocks - 1) * tap_count, chan_count)


def local(tokens, embed_table, norm_gain, w_in, short_taps, filters, w_out):
    token_ids = tokens[0]
    own_len = token_ids.shape[0]
    tap_count = filters.shape[1]
    table_vals = embed_table.astype(jnp.float32)
    square_sums = lax.psum(jnp.sum(table_vals * table_vals, axis=1, keepdims=True), "wt")
    feature_count = embed_table.shape[1] * lax.axis_size("wt")
    row_scale = lax.rsqrt(square_sums / feature_count + 1e-06)
    normed = (table_vals * row_scale * norm_gain.astype(jnp.float32)).astype(jnp.bfloat16)
    local_chans = w_in.shape[2]
    w_flat = w_in.reshape(w_in.shape[0], 3 * local_chans)
    vocab_size = embed_table.shape[0]
    partial_sum = jnp.dot(normed, w_flat, preferred_element_type=jnp.float32)
    vocab_flat = lax.psum(partial_sum, "wt").astype(jnp.bfloat16)
    vocab_proj = vocab_flat.reshape(vocab_size, 3, local_chans)
    vocab_all, tap_all, filter_all = (
        lax.all_gather(vocab_proj, "seq", axis=2, tiled=True),
        lax.all_gather(short_taps, "seq", axis=2, tiled=True),
        lax.all_gather(filters, "seq", axis=0, tiled=True),
    )
    projected = jnp.take(vocab_all, token_ids, axis=0)
    edge_prev = shifted(projected[own_len - 2 :], "seq", 1)
    mixture = short_mix(
        jnp.concatenate([edge_prev, projected], axis=0), tap_all.astype(jnp.float32)
    )
    product = (mixture[:, 0] * mixture[:, 2]).astype(jnp.bfloat16)
    tail_prev = shifted(product[own_len - tap_count + 1 :], "seq", 1)
    chan_count = product.shape[1]
    extended = jnp.concatenate(
        [jnp.zeros((1, chan_count), jnp.bfloat16), tail_prev, product], axis=0
    )
    lower_mat, upper_mat = causal_pair(filter_all)
    filtered = run_filter(extended, lower_mat, upper_mat)
    gated = (mixture[:, 1] * filtered).astype(jnp.bfloat16)
    everyone = lax.all_gather(tokens, "wt", axis=0, tiled=True)
    branch = jnp.einsum(
        "knc,dc->knd",
        lax.all_gather(gated[None], "wt", axis=0, tiled=True),
        w_out,
        preferred_element_type=jnp.float32,
    )
    embedded = jnp.take(embed_table, everyone, axis=0)
    return (embedded.astype(jnp.float32) + branch).astype(jnp.bfloat16)


def solution(mesh):
    placed = (
        P("wt", "seq"),
        P(None, "wt"),
        P("wt"),
        P("wt", None, "seq"),
        P(None, None, "seq"),
        P("seq", None),
        P("wt", None),
    )
    return jax.shard_map(
        local, mesh=mesh, in_specs=placed, out_specs=P(None, "seq", "wt"), check_vma=False
    )
```

profile of v0, /device:TPU:1, one launch (start us, length us, event | category | flops | bytes accessed | tf_op | source)
XLA Modules:
  0.0 520.0 jit_solution(13024097358544034017)
XLA Ops:
  6.5 1.4 copy.31
  7.9 0.0 copy-start.2
  8.0 0.0 copy-start.4
  8.0 1.5 fusion.4
  9.5 21.6 %psum.14 = f32[512,1]{0,1:T(1,128)S(1)} all-reduce(f32[512,1]{0,1:T(1,128)S(1)} %bitcast.66), channel_id=1, replica_groups=mesh['seq'=32,'wt'=8] {'wt'}, use_global_device_ids=true, to_apply=%region_1.0 | all-reduce | flops 512 | bytes 4096 | tf_op jit(solution)/shard_map/psum | solution.py:57
  31.1 0.7 convert_element_type.45
  31.8 2.0 fusion.12
  33.8 42.2 %all-reduce.2 = bf16[512,384]{1,0:T(8,128)(2,1)S(1)} all-reduce(f32[512,384]{1,0:T(8,128)S(1)} %fusion.12), channel_id=1, replica_groups=mesh['seq'=32,'wt'=8] {'wt'}, use_global_device_ids=true, to_apply=%region_2.0 | all-reduce | flops 196608 | bytes 1179648 | tf_op jit(solution)/shard_map/psum | solution.py:65
  75.9 0.2 copy.32
  76.1 1.1 copy.33
  77.2 0.0 all-gather.4.cloned.1.call-update
  77.2 0.0 all-gather.6.cloned.1.call-start
  77.3 48.3 %all_gather.16 = bf16[3,3,4096]{2,1,0:T(4,128)(2,1)S(1)} all-gather(bf16[3,3,128]{2,1,0:T(4,128)(2,1)S(1)} %copy-done.2), channel_id=1, replica_groups=mesh['seq'=32,'wt'=8] {'seq'}, dimensions={2}, use_global_device_ids=true | all-gather | bytes 76032 | tf_op jit(solution)/shard_map/all_gather | solution.py:69
  125.7 85.9 %all-gather.4.cloned.1.call-done = bf16[512,3,4096]{2,1,0:T(4,128)(2,1)} async-done(((bf16[512,3,128]{2,1,0:T(4,128)(2,1)}), bf16[512,3,4096]{2,1,0:T(4,128)(2,1)}) %all-gather.4.cloned.1.call-update) | async-done | bytes 12582928 | tf_op jit(solution)/shard_map/all_gather | solution.py:68
  211.6 13.3 %gather_fusion.1 = bf16[128,3,4096]{2,1,0:T(4,128)(2,1)} fusion(bf16[512,3,4096]{2,1,0:T(4,128)(2,1)} %all-gather.4.cloned.1.call-done, s32[1024]{0:T(1024)S(1)} %pad_clamp_fusion), kind=kCustom, calls=%fused_computation.1 | custom fusion | bytes 6291968 | tf_op jit(solution)/shard_map/jit(_take)/gather | solution.py:72
  224.9 4.3 broadcast_select_fusion.2
  229.2 2.1 copy-done.1
  231.3 2.2 collective-permute-start
  233.5 31.3 %all_gather.18 = bf16[256,128]{1,0:T(8,128)(2,1)S(1)} all-gather(bf16[8,128]{1,0:T(8,128)(2,1)S(1)} %copy-done.3), channel_id=1, replica_groups=mesh['seq'=32,'wt'=8] {'seq'}, dimensions={0}, use_global_device_ids=true | all-gather | bytes 67584 | tf_op jit(solution)/shard_map/all_gather | solution.py:70
  264.8 0.1 copy.35
  264.9 6.0 %tile.8 = bf16[256,255,128]{0,2,1:T(8,128)(2,1)} broadcast(bf16[256,128]{0,1:T(8,128)(2,1)S(1)} %copy.35), dimensions={0,2} | broadcast | bytes 16777216 | tf_op jit(solution)/shard_map/tile | solution.py:16
  270.9 19.0 %tile.9 = bf16[256,128,255]{0,2,1:T(8,128)(2,1)} reshape(bf16[256,255,128]{0,2,1:T(8,128)(2,1)} %tile.8) | data formatting | bytes 33423360 | tf_op jit(solution)/shard_map/tile | solution.py:16
  289.9 0.0 collective-permute-done
  289.9 4.7 maximum_convert_fusion
  294.6 0.0 slice-start
  294.6 0.0 slice-start.1
  294.6 9.4 %fusion = f32[128,3,4096]{2,1,0:T(4,128)} fusion(f32[130,3,4096]{2,1,0:T(4,128)S(1)} %maximum_convert_fusion, f32[3,4096]{1,0:T(4,128)S(1)} %get-tuple-element.8, f32[3,4096]{1,0:T(4,128)S(1)} %get-tuple-element.9, f32[3,4096]{1,0:T(4,128)S(1)} %get-tuple-element.7), kind=kLoop, calls=%fused_computation.4 | loop fusion | flops 7864320 | bytes 25313280 | tf_op jit(solution)/shard_map/add | solution.py:31
  303.9 9.2 %fusion.7 = bf16[128,1,4096]{2,1,0:T(2,128)(2,1)S(1)} fusion(f32[128,3,4096]{2,1,0:T(4,128)} %fusion), kind=kLoop, calls=%fused_computation.21 | loop fusion | flops 1048576 | bytes 5242880 | tf_op jit(solution)/shard_map/convert_element_type | solution.py:77
  313.2 2.1 slice.72
  315.3 2.1 copy.44
  317.4 3.4 collective-permute-start.1
  320.9 6.1 %broadcast_select_fusion = (bf16[256,128,128]{0,1,2:T(8,128)(2,1)}, bf16[256,128,128]{0,1,2:T(8,128)(2,1)}) fusion(pred[128,128]{0,1:T(8,128)(4,1)S(1)} %iota_compare_fusion, bf16[256,128,255]{0,2,1:T(8,128)(2,1)S(1)} %bitcast.57), kind=kLoop, calls=%fused_computation.10 | loop fusion | flops 8388608 | bytes 25182208 | tf_op jit(solution)/shard_map/jit(_where)/select_n | solution.py:24
  327.0 13.5 %copy.36 = bf16[256,128,128]{2,1,0:T(8,128)(2,1)} copy(bf16[256,128,128]{0,1,2:T(8,128)(2,1)} %get-tuple-element.6) | data formatting | bytes 16777216 | tf_op jit(solution)/shard_map/jit(_where)/select_n | solution.py:24
  340.5 13.5 %copy.38 = bf16[256,128,128]{2,1,0:T(8,128)(2,1)} copy(bf16[256,128,128]{0,1,2:T(8,128)(2,1)} %get-tuple-element.5) | data formatting | bytes 16777216 | tf_op jit(solution)/shard_map/jit(_where)/select_n | solution.py:24
  354.0 2.6 copy.34
  356.6 6.8 %fusion.17 = f32[256,16,128]{2,1,0:T(8,128)S(1)} fusion(bf16[128,256,16]{0,2,1:T(8,128)(2,1)S(1)} %bitcast.59, bf16[256,128,128]{2,1,0:T(8,128)(2,1)} %copy.36), kind=kOutput, calls=%fused_computation.43 | convolution fusion | flops 134217728 | bytes 11534336 | tf_op jit(solution)/shard_map/gij,bjgc->bigc/dot_general | solution.py:43
  363.4 1.7 copy.42
  365.1 0.4 concatenate.8.clone
  365.5 9.2 %convolution_add_fusion = f32[256,16,128]{2,1,0:T(8,128)} fusion(f32[256,16,128]{2,1,0:T(8,128)S(1)} %fusion.17, bf16[128,256,16]{0,2,1:T(8,128)(2,1)S(1)} %bitcast.60, bf16[256,128,128]{2,1,0:T(8,128)(2,1)} %copy.38), kind=kOutput, calls=%fused_computation.25 | convolution fusion | flops 134742016 | bytes 13631488 | tf_op jit(solution)/shard_map/gij,bjgc->bigc/dot_general | solution.py:46
  374.6 4.9 copy.39
  379.5 0.0 copy-start
  379.5 6.8 %fusion.9 = bf16[1,128,4096]{2,0,1:T(2,128)(2,1)S(1)} fusion(f32[1,128,4096]{2,0,1:T(1,128)S(1)} %copy.39, f32[128,3,4096]{2,1,0:T(4,128)} %fusion), kind=kLoop, calls=%fused_computation.24 | loop fusion | flops 1048576 | bytes 5242880 | tf_op jit(solution)/shard_map/convert_element_type | solution.py:85
  386.3 2.1 copy.40
  388.4 0.0 all-gather.6.cloned.1.call-update
  388.5 18.7 %all-gather = s32[8,1,128]{2,1,0:T(1,128)S(1)} all-gather(s32[1,1,128]{2,1,0:T(1,128)S(1)} %bitcast.68), channel_id=1, replica_groups=mesh['seq'=32,'wt'=8] {'wt'}, dimensions={0}, use_global_device_ids=true | all-gather | bytes 4608 | tf_op jit(solution)/shard_map/all_gather | solution.py:86
  407.1 4.1 gather_fusion
  411.2 87.2 %all-gather.6.cloned.1.call-done = bf16[8,128,4096]{2,1,0:T(8,128)(2,1)} async-done(((bf16[1,128,4096]{2,1,0:T(8,128)(2,1)}), bf16[8,128,4096]{2,1,0:T(8,128)(2,1)}) %all-gather.6.cloned.1.call-update) | async-done | bytes 8388624 | tf_op jit(solution)/shard_map/all_gather | solution.py:89
  498.4 14.7 %add_convert_fusion = bf16[8,128,1024]{2,1,0:T(8,128)(2,1)} fusion(bf16[8,128,1024]{2,1,0:T(8,128)(2,1)S(1)} %bitcast.61, pred[8,128]{1,0:T(8,128)(4,1)S(1)} %compare_and_fusion, bf16[8,128,4096]{2,1,0:T(8,128)(2,1)} %all-gather.6.cloned.1.call-done, bf16[1024,4096]{1,0:T(8,128)(2,1)} %param.13), kind=kOutput, calls=%fused_computation.13 | convolution fusion | flops 8594128896 | bytes 20972544 | tf_op jit(solution)/shard_map/knc,dc->knd/dot_general | solution.py:87
  (25 shorter events, 0.2 us)
Async XLA Ops:
  6.5 205.1 %all-gather.4.cloned.1.call-start = ((), (), s32[]{:S(2)}) async-start(), calls=%async_computation | async-start | bytes 17301504 | tf_op jit(solution)/shard_map/all_gather | solution.py:68
  7.9 69.3 %copy-start.2 = (bf16[3,3,128]{2,1,0:T(4,128)(2,1)S(1)}, bf16[3,3,128]{2,1,0:T(4,128)(2,1)}, u32[]{:S(2)}) copy-start(bf16[3,3,128]{2,1,0:T(4,128)(2,1)} %param.11) | copy-start | bytes 6916
  8.0 117.6 %copy-start.4 = (s32[1,128]{1,0:T(1,128)S(1)}, s32[1,128]{1,0:T(1,128)}, u32[]{:S(2)}) copy-start(s32[1,128]{1,0:T(1,128)} %param.7) | copy-start | bytes 1540
  77.2 421.2 %all-gather.6.cloned.1.call-start = ((), (), s32[]{:S(2)}) async-start(), calls=%async_computation.1 | async-start | bytes 9437184 | tf_op jit(solution)/shard_map/all_gather | solution.py:89
  224.9 8.6 %copy-start.3 = (bf16[8,128]{1,0:T(8,128)(2,1)S(1)}, bf16[8,128]{1,0:T(8,128)(2,1)}, u32[]{:S(2)}) copy-start(bf16[8,128]{1,0:T(8,128)(2,1)} %param.12) | copy-start | bytes 6148
  229.2 2.1 copy-start.1
  231.3 58.6 %collective-permute-start = (bf16[2,3,4096]{2,1,0:T(4,128)(2,1)S(1)}, bf16[2,3,4096]{2,1,0:T(4,128)(2,1)S(1)}, u32[]{:S(2)}, u32[]{:S(2)}) collective-permute-start(bf16[2,3,4096]{2,1,0:T(4,128)(2,1)S(1)} %slice.62), channel_id=1, source_target_pairs={{0,8},{8,16},{16,24},{24,32},{32,40},{40,48},{48,56},{56,64},{64,7... | collective-permute-start | bytes 147464 | tf_op jit(solution)/shard_map/ppermute | solution.py:10
  294.6 26.3 %slice-start = ((s8[16777216]{0:T(1024)(128)(4,1)}), s8[4194304]{0:T(1024)(128)(4,1)S(1)}, s32[]{:S(2)}) async-start(s8[16777216]{0:T(1024)(128)(4,1)} %bitcast.56), calls=%async_computation.2 | async-start | bytes 8388608
  294.6 26.3 %slice-start.1 = ((s8[16777216]{0:T(1024)(128)(4,1)}), s8[4194304]{0:T(1024)(128)(4,1)S(1)}, s32[]{:S(2)}) async-start(s8[16777216]{0:T(1024)(128)(4,1)} %bitcast.56), calls=%async_computation.3 | async-start | bytes 8388608
  294.6 26.3 %slice-start.2 = ((s8[16777216]{0:T(1024)(128)(4,1)}), s8[4194304]{0:T(1024)(128)(4,1)S(1)}, s32[]{:S(2)}) async-start(s8[16777216]{0:T(1024)(128)(4,1)} %bitcast.56), calls=%async_computation.4 | async-start | bytes 8388608
  303.9 16.9 %slice-start.3 = ((s8[16777216]{0:T(1024)(128)(4,1)}), s8[4194304]{0:T(1024)(128)(4,1)S(1)}, s32[]{:S(2)}) async-start(s8[16777216]{0:T(1024)(128)(4,1)} %bitcast.56), calls=%async_computation.5 | async-start | bytes 8388608
  317.4 46.0 %collective-permute-start.1 = (bf16[127,4096]{1,0:T(8,128)(2,1)}, bf16[127,4096]{1,0:T(8,128)(2,1)}, u32[]{:S(2)}, u32[]{:S(2)}) collective-permute-start(bf16[127,4096]{1,0:T(8,128)(2,1)} %bitcast.55), channel_id=1, source_target_pairs={{0,8},{8,16},{16,24},{24,32},{32,40},{40,48},{48,56},{56,64},{64,7... | collective-permute-start | bytes 3121160 | tf_op jit(solution)/shard_map/ppermute | solution.py:10
  379.5 27.6 %copy-start = (bf16[512,1024]{1,0:T(8,128)(2,1)S(1)}, bf16[512,1024]{1,0:T(8,128)(2,1)}, u32[]{:S(2)}) copy-start(bf16[512,1024]{1,0:T(8,128)(2,1)} %param.8) | copy-start | bytes 3145732
Sparse Core Ops, SparseCore 0:
  77.3 134.2 all-gather.3
  388.6 109.8 all-gather.5
where the time goes:
time: 522 us; the launch traced here: 520 us
  waiting for transfers between devices  173 us (33%)
  blocking collectives  162 us (31%)
  local copies, waits for them, and re-layouts  90.2 us (17%)
  other arithmetic  42.6 us (8%)
  matrix products  32.6 us (6%)
  between operations  13.7 us (3%)
  starting transfers between devices  5.65 us (1%)
    all_gather x1, waiting for transfers between devices, local(): lax.all_gather(gated[None], 'wt', axis=0, tiled=True)  87.2 us
    all_gather x1, waiting for transfers between devices, local(): lax.all_gather(vocab_proj, 'seq', axis=2, tiled=True)  85.9 us
    all_gather x1, blocking collectives, local(): lax.all_gather(short_taps, 'seq', axis=2, tiled=True)  48.3 us
    psum x1, blocking collectives, local(): vocab_flat = lax.psum(partial_sum, 'wt').astype(jnp.bfloat16)  42.2 us
    all_gather x1, blocking collectives, local(): lax.all_gather(filters, 'seq', axis=0, tiled=True)  31.3 us
    another operation x2, local copies, waits for them, and re-layouts, causal_pair(): jnp.tile(filter_vals, (1, 2 * tap_count - 1))  25 us
    psum x1, blocking collectives, local(): lax.psum(jnp.sum(table_vals * table_vals, axis=1, keepdims=True), 'wt')  21.6 us
    all_gather x1, blocking collectives, local(): everyone = lax.all_gather(tokens, 'wt', axis=0, tiled=True)  18.7 us
  transfers between devices with their start and end apart: 4, of which 2 were waited for; matrix products, arithmetic and copies ran while one was open for 14% of the time, Pallas kernels for 0%

commit v1 on v0

v1 whole, which is shorter than its diff:
```python
import functools

import jax
import jax.numpy as jnp
from jax import lax
from jax.experimental import pallas as pl
from jax.experimental.pallas import tpu as pltpu
from jax.sharding import PartitionSpec as P

F32 = jnp.float32
BF16 = jnp.bfloat16
BLK = 128
GSZ = 16
RING = 4
WT = 2 * RING


def block_kernel(
    nseq,
    feature_count,
    tok_ref,
    emb_ref,
    gain_ref,
    win_ref,
    taps_ref,
    base_ref,
    wout_hbm,
    out_ref,
    wout,
    part_out,
    part_in,
    sq_out,
    sq_in,
    vtab,
    tok_seq,
    tok_wt,
    toep,
    ext,
    carry,
    sbuf,
    gath,
    acc,
    wout_sem,
    self_sem,
    p_send,
    p_recv,
    q_send,
    q_recv,
    v_send,
    v_recv,
    ts_send,
    ts_recv,
    tw_send,
    tw_recv,
    s1,
    r1,
    sx,
    rx,
    sy,
    ry,
):
    nchip = nseq // 2
    seq = lax.axis_index("seq")
    wt = lax.axis_index("wt")
    chip, core = seq // 2, seq % 2
    y, xh = wt // 2, wt % 2
    vocab = emb_ref.shape[0]
    vrow = vocab // WT
    wide = 3 * BLK

    def genome(dy, flip):
        return ((y + dy + RING) % RING) * 2 + (xh if flip == 0 else 1 - xh)

    def remote(src, dst, ssem, rsem, where):
        return pltpu.make_async_remote_copy(
            src_ref=src,
            dst_ref=dst,
            send_sem=ssem,
            recv_sem=rsem,
            device_id=where,
            device_id_type=pl.DeviceIdType.MESH,
        )

    def seq_peer(d):
        return {"seq": (seq + d) % nseq}

    def wt_peer(d):
        return {"wt": (wt + d) % WT}

    barrier = pltpu.get_barrier_semaphore()

    @pl.loop(1, nseq)
    def _(d):
        pl.semaphore_signal(
            barrier, inc=1, device_id=seq_peer(d), device_id_type=pl.DeviceIdType.MESH
        )

    @pl.loop(1, WT)
    def _(d):
        pl.semaphore_signal(
            barrier, inc=1, device_id=wt_peer(d), device_id_type=pl.DeviceIdType.MESH
        )

    load_wout = pltpu.make_async_copy(wout_hbm, wout, wout_sem)
    load_wout.start()

    sq_out[...] = jnp.zeros_like(sq_out)
    rows = vocab // 2

    @pl.loop(0, 2)
    def _(i):
        e = emb_ref[pl.ds(pl.multiple_of(i * rows, rows), rows), :].astype(F32)
        sq = jnp.sum(e * e, axis=1, keepdims=True)
        r = lax.broadcasted_iota(jnp.int32, (rows, vocab), 0) + i * rows
        l = lax.broadcasted_iota(jnp.int32, (rows, vocab), 1)
        sq_out[...] += jnp.sum(jnp.where(r == l, sq, 0.0), axis=0, keepdims=True)
        gained = (e * gain_ref[...].astype(F32)).astype(BF16)
        p = jnp.dot(gained, win_ref[...], preferred_element_type=F32).astype(BF16)
        for k in range(WT // 2):
            part_out[i * (WT // 2) + k] = p[k * vrow : (k + 1) * vrow]

    tok_seq[seq] = tok_ref[...]
    tok_wt[wt] = tok_ref[...]

    pl.semaphore_wait(barrier, nseq - 1 + WT - 1)

    def part_copy(d):
        return remote(
            part_out.at[(wt + d) % WT], part_in.at[d], p_send.at[d], p_recv.at[d], wt_peer(d)
        )

    def sq_copy(d):
        return remote(sq_out, sq_in.at[d], q_send.at[d], q_recv.at[d], wt_peer(d))

    def tok_wt_copy(d):
        return remote(tok_ref, tok_wt.at[wt], tw_send.at[d], tw_recv.at[d], wt_peer(d))

    def tok_seq_copy(d):
        return remote(tok_ref, tok_seq.at[seq], ts_send.at[d], ts_recv.at[d], seq_peer(d))

    @pl.loop(1, WT)
    def _(d):
        sq_copy(d).start()
        part_copy(d).start()

    @pl.loop(1, WT)
    def _(d):
        tok_wt_copy(d).start()

    @pl.loop(1, nseq)
    def _(d):
        tok_seq_copy(d).start()

    @pl.loop(0, BLK // GSZ)
    def _(q):
        row = jnp.broadcast_to(base_ref[pl.ds(q, 1), :], (BLK, 2 * BLK))
        toep[pl.ds(pl.multiple_of(q * BLK, BLK), BLK), :] = pltpu.roll(
            row, 0, 1, stride=1, stride_axis=0
        ).astype(BF16)

    @pl.loop(1, WT)
    def _(d):
        sq_copy(d).wait_recv()
        part_copy(d).wait_recv()

    total = part_out[wt].astype(F32)
    squares = sq_out[...]
    for d in range(1, WT):
        total = total + part_in[d].astype(F32)
        squares = squares + sq_in[d]
    scale = lax.rsqrt(squares / feature_count + 1e-06)
    r = lax.broadcasted_iota(jnp.int32, (vrow, vocab), 0) + wt * vrow
    l = lax.broadcasted_iota(jnp.int32, (vrow, vocab), 1)
    scale_col = jnp.sum(jnp.where(r == l, scale, 0.0), axis=1, keepdims=True)
    vtab[wt] = (total * scale_col).astype(BF16)

    def vocab_copy(d):
        return remote(vtab.at[wt], vtab.at[wt], v_send.at[d], v_recv.at[d], wt_peer(d))

    def vocab_arrival(d):
        whence = (wt - d + WT) % WT
        return remote(
            vtab.at[whence], vtab.at[whence], v_send.at[d], v_recv.at[d], wt_peer(d)
        )

    @pl.loop(1, WT)
    def _(d):
        vocab_copy(d).start()

    def one_hot(row):
        cols = jnp.broadcast_to(row, (BLK, BLK)).T
        lane = lax.broadcasted_iota(jnp.int32, (BLK, BLK), 1)
        return jnp.concatenate(
            [
                jnp.where(cols == lane + k * BLK, 1.0, 0.0).astype(BF16)
                for k in range(vocab // BLK)
            ],
            axis=1,
        )

    @pl.loop(1, WT)
    def _(d):
        whence = (wt - d + WT) % WT
        remote(
            tok_ref, tok_wt.at[whence], tw_send.at[d], tw_recv.at[d], wt_peer(d)
        ).wait_recv()

    @pl.loop(0, WT // 2)
    def _(g):
        hot = jnp.concatenate([one_hot(tok_wt[2 * g]), one_hot(tok_wt[2 * g + 1])], axis=0)
        acc[pl.ds(pl.multiple_of(g * 2 * BLK, 2 * BLK), 2 * BLK), :] = jnp.dot(
            hot, emb_ref[...], preferred_element_type=F32
        )

    @pl.loop(1, nseq)
    def _(d):
        whence = (seq - d + nseq) % nseq
        remote(
            tok_ref, tok_seq.at[whence], ts_send.at[d], ts_recv.at[d], seq_peer(d)
        ).wait_recv()

    load_wout.wait()

    @pl.loop(1, WT)
    def _(d):
        vocab_arrival(d).wait_recv()

    ext[...] = jnp.zeros_like(ext)
    carry[...] = jnp.zeros_like(carry)

    def block_send(u, i):
        to = 2 * ((chip + u) % nchip) + i
        return remote(
            sbuf.at[u, i],
            gath.at[u, wt, :, pl.ds(pl.multiple_of(core * BLK, BLK), BLK)],
            s1.at[u, i],
            r1.at[u, core],
            {"seq": to},
        )

    def block_local(i):
        return pltpu.make_async_copy(
            sbuf.at[0, i],
            gath.at[0, wt, :, pl.ds(pl.multiple_of(core * BLK, BLK), BLK)],
            self_sem,
        )

    def block_arrival(u, i):
        return remote(
            sbuf.at[u, i],
            gath.at[u, wt, :, pl.ds(i * BLK, BLK)],
            s1.at[u, i],
            r1.at[u, i],
            {"seq": 2 * ((chip + u) % nchip) + i},
        )

    def mixer(u):
        at = (chip + u + nchip) % nchip

        @pl.when(at == 0)
        def _():
            ext[0:8, :] = jnp.zeros((8, wide), F32)
            carry[...] = jnp.zeros_like(carry)

        hot = jnp.concatenate([one_hot(tok_seq[2 * at]), one_hot(tok_seq[2 * at + 1])], axis=0)
        ext[8 : 8 + 2 * BLK, :] = jnp.dot(
            hot, vtab[...].reshape(vocab, wide), preferred_element_type=F32
        )

        def mixed(s):
            lanes = slice(s * BLK, (s + 1) * BLK)
            return (
                taps_ref[0:1, lanes] * ext[8 : 8 + 2 * BLK, lanes]
                + taps_ref[1:2, lanes] * ext[7 : 7 + 2 * BLK, lanes]
                + taps_ref[2:3, lanes] * ext[6 : 6 + 2 * BLK, lanes]
            )

        inner = (mixed(0) * mixed(2)).astype(BF16)
        middle = mixed(1)
        first, second = inner[:BLK], inner[BLK:]
        pair = jnp.concatenate(
            [
                jnp.concatenate([carry[...], first], axis=1),
                jnp.concatenate([first, second], axis=1),
            ],
            axis=0,
        )
        filtered = jnp.dot(toep[...], pair, preferred_element_type=F32)
        group = (lax.broadcasted_iota(jnp.int32, (BLK, 2 * BLK), 1) % BLK) // GSZ
        conv = filtered[0:BLK]
        for q in range(1, BLK // GSZ):
            conv = jnp.where(group == q, filtered[q * BLK : (q + 1) * BLK], conv)
        carry[...] = second
        ext[0:8, :] = ext[2 * BLK : 2 * BLK + 8, :]

        @pl.when(u >= 0)
        def _():
            sbuf[u, 0] = (middle[:BLK] * conv[:, :BLK]).astype(BF16)
            sbuf[u, 1] = (middle[BLK:] * conv[:, BLK:]).astype(BF16)
            for i in range(2):
                mine = (u == 0) & (core == i)

                @pl.when(mine)
                def _():
                    block_local(i).start()

                @pl.when(jnp.logical_not(mine))
                def _():
                    block_send(u, i).start()

    def x_copy(u, g):
        return remote(
            gath.at[u, g], gath.at[u, g], sx.at[u], rx.at[u], {"wt": genome(0, 1)}
        )

    def y_copy(u, way, kind, g):
        k = (u * 2 + way) * 3 + kind
        to = genome(1 if way == 0 else -1, 0)
        return remote(gath.at[u, g], gath.at[u, g], sy.at[k], ry.at[k], {"wt": to})

    def spread(u):
        for i in range(2):
            mine = (u == 0) & (core == i)

            @pl.when(mine)
            def _():
                block_local(i).wait()

            @pl.when(jnp.logical_not(mine))
            def _():
                block_arrival(u, i).wait_recv()

        y_copy(u, 0, 0, wt).start()
        y_copy(u, 1, 0, wt).start()
        x_copy(u, wt).start()

    def spread_partner(u):
        other = genome(0, 1)
        x_copy(u, other).wait_recv()
        y_copy(u, 0, 1, other).start()
        y_copy(u, 1, 1, other).start()

    def relay(u):
        behind = genome(-1, 0)
        y_copy(u, 0, 0, behind).wait_recv()
        y_copy(u, 0, 2, behind).start()
        ahead = genome(1, 1)
        y_copy(u, 1, 1, ahead).wait_recv()
        y_copy(u, 1, 2, ahead).start()

    def project(u):
        y_copy(u, 0, 1, genome(-1, 1)).wait_recv()
        y_copy(u, 1, 0, genome(1, 0)).wait_recv()
        y_copy(u, 0, 2, genome(-2, 0)).wait_recv()
        y_copy(u, 1, 2, genome(2, 1)).wait_recv()
        owner = (chip - u + nchip) % nchip
        cols = pl.ds(pl.multiple_of(owner * 2 * BLK, 2 * BLK), 2 * BLK)
        held = gath[u].reshape(WT * BLK, 2 * BLK)
        tile = min(256, acc.shape[1])

        @pl.loop(0, acc.shape[1] // tile)
        def _(n):
            at = pl.ds(pl.multiple_of(n * tile, tile), tile)
            acc[:, at] += lax.dot_general(
                held, wout[at, cols], (((1,), (1,)), ((), ())), preferred_element_type=F32
            )

    @pl.loop(-1, nchip + 4)
    def _(t):
        @pl.when(t < nchip)
        def _():
            mixer(t)

        for lag, stage in ((1, spread), (2, spread_partner), (3, relay), (4, project)):

            @pl.when((t >= lag) & (t < nchip + lag))
            def _():
                stage(t - lag)

    @pl.loop(0, WT)
    def _(g):
        out_ref[g] = acc[pl.ds(pl.multiple_of(g * BLK, BLK), BLK), :].astype(BF16)

    @pl.loop(1, WT)
    def _(d):
        sq_copy(d).wait_send()
        part_copy(d).wait_send()
        tok_wt_copy(d).wait_send()
        vocab_copy(d).wait_send()

    @pl.loop(1, nseq)
    def _(d):
        tok_seq_copy(d).wait_send()

    @pl.loop(0, nchip)
    def _(u):
        for i in range(2):

            @pl.when(jnp.logical_not((u == 0) & (core == i)))
            def _():
                block_send(u, i).wait_send()

        x_copy(u, wt).wait_send()
        for kind in range(3):
            for way in range(2):
                y_copy(u, way, kind, wt).wait_send()


def local(nseq, tokens, embed_table, norm_gain, w_in, short_taps, filters, w_out):
    vocab, feats = embed_table.shape
    taps = filters.shape[1]
    base = jnp.pad(filters[:, ::-1].astype(F32), ((0, 0), (1, taps - 1)))
    nchip = nseq // 2
    wide = 3 * BLK
    dma = pltpu.SemaphoreType.DMA
    vmem = pl.BlockSpec(memory_space=pltpu.VMEM)
    return pl.pallas_call(
        functools.partial(block_kernel, nseq, feats * WT),
        out_shape=jax.ShapeDtypeStruct((WT, BLK, feats), BF16),
        in_specs=[vmem] * 6 + [pl.BlockSpec(memory_space=pl.ANY)],
        out_specs=vmem,
        scratch_shapes=[
            pltpu.VMEM(w_out.shape, BF16),
            pltpu.VMEM((WT, vocab // WT, wide), BF16),
            pltpu.VMEM((WT, vocab // WT, wide), BF16),
            pltpu.VMEM((1, vocab), F32),
            pltpu.VMEM((WT, 1, vocab), F32),
            pltpu.VMEM((WT, vocab // WT, wide), BF16),
            pltpu.VMEM((nseq, 1, BLK), jnp.int32),
            pltpu.VMEM((WT, 1, BLK), jnp.int32),
            pltpu.VMEM((BLK // GSZ * BLK, 2 * BLK), BF16),
            pltpu.VMEM((8 + 2 * BLK, wide), F32),
            pltpu.VMEM((BLK, BLK), BF16),
            pltpu.VMEM((nchip, 2, BLK, BLK), BF16),
            pltpu.VMEM((nchip, WT, BLK, 2 * BLK), BF16),
            pltpu.VMEM((WT * BLK, feats), F32),
            dma,
            dma,
            dma((WT,)),
            dma((WT,)),
            dma((WT,)),
            dma((WT,)),
            dma((WT,)),
            dma((WT,)),
            dma((nseq,)),
            dma((nseq,)),
            dma((WT,)),
            dma((WT,)),
            dma((nchip, 2)),
            dma((nchip, 2)),
            dma((nchip,)),
            dma((nchip,)),
            dma((nchip * 6,)),
            dma((nchip * 6,)),
        ],
        compiler_params=pltpu.CompilerParams(collective_id=0, has_side_effects=True),
        name="hyena_block",
    )(
        tokens,
        embed_table,
        norm_gain.reshape(1, feats),
        w_in.reshape(feats, wide),
        short_taps.astype(F32).reshape(3, wide),
        base,
        w_out,
    )


def solution(mesh):
    placed = (
        P("wt", "seq"),
        P(None, "wt"),
        P("wt"),
        P("wt", None, "seq"),
        P(None, None, "seq"),
        P("seq", None),
        P("wt", None),
    )
    return jax.shard_map(
        functools.partial(local, mesh.shape["seq"]),
        mesh=mesh,
        in_specs=placed,
        out_specs=P(None, "seq", "wt"),
        check_vma=False,
    )
```

time: 522 us -> 127 us (0.24)
  waiting for transfers between devices: 173 us -> 0 us
  blocking collectives: 162 us -> 0 us
  Pallas kernels: 0 us -> 116 us
  local copies, waits for them, and re-layouts: 90.2 us -> 8.27 us
  other arithmetic: 42.6 us -> 1.35 us
  matrix products: 32.6 us -> 0 us
  between operations: 13.7 us -> 0.02 us
  starting transfers between devices: 5.65 us -> 0 us
    all_gather x2 -> x0, waiting for transfers between devices: 173 us -> none  [the longest x1 87.2 us: local(): lax.all_gather(gated[None], 'wt', axis=0, tiled=True)]
    pallas_call x0 -> x1, Pallas kernels: none -> 116 us  [local(): pl.pallas_call(functools.partial(block_kernel, nseq, feats * WT), out_sha...]
    all_gather x3 -> x0, blocking collectives: 98.2 us -> none  [the longest x1 48.3 us: local(): lax.all_gather(short_taps, 'seq', axis=2, tiled=True)]
    psum x2 -> x0, blocking collectives: 63.7 us -> none  [the longest x1 42.2 us: local(): vocab_flat = lax.psum(partial_sum, 'wt').astype(jnp.bfloat16)]
    dot_general x4 -> x0, matrix products: 32.6 us -> none  [the longest x1 14.7 us: local(): jnp.einsum('knc,dc->knd', lax.all_gather(gated[None], 'wt', axis=0, tiled...]
    select_n x2 -> x0, local copies, waits for them, and re-layouts: 27 us -> none  [the longest x1 13.5 us: causal_pair(): jnp.where(lower_mask, circulant, zero_mat)]
    another operation x2 -> x0, local copies, waits for them, and re-layouts: 25 us -> none  [causal_pair(): jnp.tile(filter_vals, (1, 2 * tap_count - 1))]
    convert_element_type x5 -> x0, other arithmetic: 21.4 us -> none  [the longest x1 9.21 us: local(): product = (mixture[:, 0] * mixture[:, 2]).astype(jnp.bfloat16)]
  transfers between devices with their start and end apart: 4 -> 0, of which waited for: 2 -> 0; matrix products, arithmetic and copies ran while one was open for 14% -> 0% of each run, Pallas kernels for 0% -> 0%
where the time goes in v1:
time: 127 us; the launch traced here: 126 us
  Pallas kernels  116 us (91%)
  local copies, waits for them, and re-layouts  8.27 us (7%)
  other arithmetic  1.35 us (1%)
    pallas_call x1, Pallas kernels, local(): pl.pallas_call(functools.partial(block_kernel, nseq, feats * WT), out_sha...  116 us
    unnamed x3, local copies, waits for them, and re-layouts  5.08 us

profile of v1, /device:TPU:1, one launch (start us, length us, event | category | flops | bytes accessed | tf_op | source)
XLA Modules:
  0.0 125.5 jit_solution(6714462060222952172)
XLA Ops:
  0.0 0.8 rev.3
  0.8 1.3 %reshape.11.gain_ref = bf16[1,1024]{1,0:T(2,128)(2,1)} reshape(bf16[1024]{0:T(1024)(128)(2,1)} %param.9) | data formatting | bytes 4096 | tf_op jit(solution)/shard_map/reshape | solution.py:461
  2.0 0.7 pad_convert_fusion.base_ref
  2.7 0.7 convert_bitcast_fusion
  3.4 0.6 copy.13
  4.0 1.4 %copy.9 = bf16[1024,3,128]{0,2,1:T(8,128)(2,1)S(1)} copy(bf16[1024,3,128]{2,0,1:T(8,128)(2,1)} %param.10) | data formatting | bytes 1572864 | tf_op args[3]
  5.4 1.2 copy.10.win_ref
  6.6 115.9 %hyena_block.1 = bf16[8,128,1024]{2,1,0:T(8,128)(2,1)} custom-call(s32[1,128]{1,0:T(1,128)} %tok_ref.1, bf16[512,1024]{1,0:T(8,128)(2,1)} %emb_ref.1, bf16[1,1024]{1,0:T(2,128)(2,1)} %reshape.11.gain_ref, bf16[1024,384]{1,0:T(8,128)(2,1)} %copy.10.win_ref, f32[3,384]{1,0:T(4,128)} %bitcast.7, f32[8,256]{1,0:T(8,128)} %pad_convert_fusion.base_ref, ...), custom_call_target="tpu_custom_call" | custom-call | tf_op jit(solution)/shard_map/hyena_block/pallas_call | solution.py:417
  122.5 3.1 %copy.15 = bf16[8,128,1024]{2,1,0:T(8,128)(2,1)} copy(bf16[8,128,1024]{2,1,0:T(8,128)(2,1)} %hyena_block.1) | data formatting | bytes 4194304

commit v2 on v1

--- a/solution.py
+++ b/solution.py
@@ -11,6 +11,7 @@
 BF16 = jnp.bfloat16
 BLK = 128
 GSZ = 16
+HALO = 16
 RING = 4
 WT = 2 * RING
 
@@ -23,7 +24,7 @@
     gain_ref,
     win_ref,
     taps_ref,
-    base_ref,
+    filt_ref,
     wout_hbm,
     out_ref,
     wout,
@@ -36,7 +37,6 @@
     tok_wt,
     toep,
     ext,
-    carry,
     sbuf,
     gath,
     acc,
@@ -59,7 +59,7 @@
     sy,
     ry,
 ):
-    nchip = nseq // 2
+    nchip, nz = nseq // 2, nseq // 4
     seq = lax.axis_index("seq")
     wt = lax.axis_index("wt")
     chip, core = seq // 2, seq % 2
@@ -114,10 +114,19 @@
         r = lax.broadcasted_iota(jnp.int32, (rows, vocab), 0) + i * rows
         l = lax.broadcasted_iota(jnp.int32, (rows, vocab), 1)
         sq_out[...] += jnp.sum(jnp.where(r == l, sq, 0.0), axis=0, keepdims=True)
-        gained = (e * gain_ref[...].astype(F32)).astype(BF16)
-        p = jnp.dot(gained, win_ref[...], preferred_element_type=F32).astype(BF16)
+        gained = (e * gain_ref[...].astype(F32).reshape(1, -1)).astype(BF16)
+        streams = jnp.concatenate([win_ref[k] for k in range(3)], axis=1)
+        p = jnp.dot(gained, streams, preferred_element_type=F32).astype(BF16)
         for k in range(WT // 2):
             part_out[i * (WT // 2) + k] = p[k * vrow : (k + 1) * vrow]
+
+    filt = filt_ref[...].astype(F32)
+    for q in range(BLK // GSZ):
+        row = jnp.concatenate([filt[q : q + 1], jnp.zeros((1, BLK), F32)], axis=1)
+        rolled = pltpu.roll(
+            jnp.broadcast_to(row, (2 * BLK, 2 * BLK)), BLK, 1, stride=1, stride_axis=0
+        )
+        toep[q * BLK : (q + 1) * BLK, :] = rolled[:, :BLK].T.astype(BF16)
 
     tok_seq[seq] = tok_ref[...]
     tok_wt[wt] = tok_ref[...]
@@ -150,13 +159,6 @@
     @pl.loop(1, nseq)
     def _(d):
         tok_seq_copy(d).start()
-
-    @pl.loop(0, BLK // GSZ)
-    def _(q):
-        row = jnp.broadcast_to(base_ref[pl.ds(q, 1), :], (BLK, 2 * BLK))
-        toep[pl.ds(pl.multiple_of(q * BLK, BLK), BLK), :] = pltpu.roll(
-            row, 0, 1, stride=1, stride_axis=0
-        ).astype(BF16)
 
     @pl.loop(1, WT)
     def _(d):
@@ -198,20 +200,6 @@
             axis=1,
         )
 
-    @pl.loop(1, WT)
-    def _(d):
-        whence = (wt - d + WT) % WT
-        remote(
-            tok_ref, tok_wt.at[whence], tw_send.at[d], tw_recv.at[d], wt_peer(d)
-        ).wait_recv()
-
-    @pl.loop(0, WT // 2)
-    def _(g):
-        hot = jnp.concatenate([one_hot(tok_wt[2 * g]), one_hot(tok_wt[2 * g + 1])], axis=0)
-        acc[pl.ds(pl.multiple_of(g * 2 * BLK, 2 * BLK), 2 * BLK), :] = jnp.dot(
-            hot, emb_ref[...], preferred_element_type=F32
-        )
-
     @pl.loop(1, nseq)
     def _(d):
         whence = (seq - d + nseq) % nseq
@@ -219,17 +207,23 @@
             tok_ref, tok_seq.at[whence], ts_send.at[d], ts_recv.at[d], seq_peer(d)
         ).wait_recv()
 
-    load_wout.wait()
-
     @pl.loop(1, WT)
     def _(d):
         vocab_arrival(d).wait_recv()
 
-    ext[...] = jnp.zeros_like(ext)
-    carry[...] = jnp.zeros_like(carry)
+    steps = [0, 2, -2, 3, -3, 4, 1, -1] if nz == 8 else list(range(nz))
+
+    def offset(u):
+        step = sum(jnp.where(u // 2 == k, v, 0) for k, v in enumerate(steps) if v != 0)
+        return u % 2, step
+
+    def chip_at(u, sign):
+        flip, step = offset(u)
+        xl, z = chip // nz, chip % nz
+        return ((xl + flip) % 2) * nz + (z + sign * step + nz) % nz
 
     def block_send(u, i):
-        to = 2 * ((chip + u) % nchip) + i
+        to = 2 * chip_at(u, 1) + i
         return remote(
             sbuf.at[u, i],
             gath.at[u, wt, :, pl.ds(pl.multiple_of(core * BLK, BLK), BLK)],
@@ -251,36 +245,35 @@
             gath.at[u, wt, :, pl.ds(i * BLK, BLK)],
             s1.at[u, i],
             r1.at[u, i],
-            {"seq": 2 * ((chip + u) % nchip) + i},
+            {"seq": 2 * chip_at(u, 1) + i},
         )
 
     def mixer(u):
-        at = (chip + u + nchip) % nchip
-
-        @pl.when(at == 0)
-        def _():
-            ext[0:8, :] = jnp.zeros((8, wide), F32)
-            carry[...] = jnp.zeros_like(carry)
-
-        hot = jnp.concatenate([one_hot(tok_seq[2 * at]), one_hot(tok_seq[2 * at + 1])], axis=0)
-        ext[8 : 8 + 2 * BLK, :] = jnp.dot(
-            hot, vtab[...].reshape(vocab, wide), preferred_element_type=F32
-        )
-
-        def mixed(s):
+        at = chip_at(u, 1)
+        before = (2 * at - 2 + nseq) % nseq
+        hot = jnp.concatenate(
+            [one_hot(tok_seq[before])[BLK - HALO :]]
+            + [one_hot(tok_seq[(before + k) % nseq]) for k in range(1, 4)],
+            axis=0,
+        )
+        proj = jnp.dot(hot, vtab[...].reshape(vocab, wide), preferred_element_type=F32)
+        past = HALO + BLK
+        ext[:past, :] = jnp.where(at > 0, proj[:past], 0.0)
+        ext[past:, :] = proj[past:]
+
+        def mixed(s, start, rows):
             lanes = slice(s * BLK, (s + 1) * BLK)
-            return (
-                taps_ref[0:1, lanes] * ext[8 : 8 + 2 * BLK, lanes]
-                + taps_ref[1:2, lanes] * ext[7 : 7 + 2 * BLK, lanes]
-                + taps_ref[2:3, lanes] * ext[6 : 6 + 2 * BLK, lanes]
+            return sum(
+                taps_ref[k][s : s + 1].astype(F32) * ext[start - k : start - k + rows, lanes]
+                for k in range(3)
             )
 
-        inner = (mixed(0) * mixed(2)).astype(BF16)
-        middle = mixed(1)
-        first, second = inner[:BLK], inner[BLK:]
+        inner = (mixed(0, HALO, 3 * BLK) * mixed(2, HALO, 3 * BLK)).astype(BF16)
+        middle = mixed(1, past, 2 * BLK)
+        prior, first, second = (inner[k * BLK : (k + 1) * BLK] for k in range(3))
         pair = jnp.concatenate(
             [
-                jnp.concatenate([carry[...], first], axis=1),
+                jnp.concatenate([prior, first], axis=1),
                 jnp.concatenate([first, second], axis=1),
             ],
             axis=0,
@@ -290,33 +283,35 @@
         conv = filtered[0:BLK]
         for q in range(1, BLK // GSZ):
             conv = jnp.where(group == q, filtered[q * BLK : (q + 1) * BLK], conv)
-        carry[...] = second
-        ext[0:8, :] = ext[2 * BLK : 2 * BLK + 8, :]
-
-        @pl.when(u >= 0)
-        def _():
-            sbuf[u, 0] = (middle[:BLK] * conv[:, :BLK]).astype(BF16)
-            sbuf[u, 1] = (middle[BLK:] * conv[:, BLK:]).astype(BF16)
-            for i in range(2):
-                mine = (u == 0) & (core == i)
-
-                @pl.when(mine)
-                def _():
-                    block_local(i).start()
-
-                @pl.when(jnp.logical_not(mine))
-                def _():
-                    block_send(u, i).start()
-
-    def x_copy(u, g):
+        sbuf[u, 0] = (middle[:BLK] * conv[:, :BLK]).astype(BF16)
+        sbuf[u, 1] = (middle[BLK:] * conv[:, BLK:]).astype(BF16)
+        for i in range(2):
+            mine = (u == 0) & (core == i)
+
+            @pl.when(mine)
+            def _():
+                block_local(i).start()
+
+            @pl.when(jnp.logical_not(mine))
+            def _():
+                block_send(u, i).start()
+
+    def x_copy(u, kind, g):
+        k = u * 4 + kind
         return remote(
-            gath.at[u, g], gath.at[u, g], sx.at[u], rx.at[u], {"wt": genome(0, 1)}
-        )
-
-    def y_copy(u, way, kind, g):
+            gath.at[u, g], gath.at[u, g], sx.at[k], rx.at[k], {"wt": genome(0, 1)}
+        )
+
+    def y_copy(u, way, kind, g, half=False):
         k = (u * 2 + way) * 3 + kind
         to = genome(1 if way == 0 else -1, 0)
-        return remote(gath.at[u, g], gath.at[u, g], sy.at[k], ry.at[k], {"wt": to})
+        part = gath.at[u, g]
+        if half:
+            part = gath.at[u, g, way * (BLK // 2) : (way + 1) * (BLK // 2)]
+        return remote(part, part, sy.at[k], ry.at[k], {"wt": to})
+
+    def late(u):
+        return u % 3 == 1
 
     def spread(u):
         for i in range(2):
@@ -332,54 +327,117 @@
 
         y_copy(u, 0, 0, wt).start()
         y_copy(u, 1, 0, wt).start()
-        x_copy(u, wt).start()
-
-    def spread_partner(u):
-        other = genome(0, 1)
-        x_copy(u, other).wait_recv()
-        y_copy(u, 0, 1, other).start()
-        y_copy(u, 1, 1, other).start()
+        x_copy(u, 0, wt).start()
 
     def relay(u):
-        behind = genome(-1, 0)
-        y_copy(u, 0, 0, behind).wait_recv()
-        y_copy(u, 0, 2, behind).start()
-        ahead = genome(1, 1)
-        y_copy(u, 1, 1, ahead).wait_recv()
-        y_copy(u, 1, 2, ahead).start()
+        @pl.when(jnp.logical_not(late(u)))
+        def _():
+            other = genome(0, 1)
+            x_copy(u, 0, other).wait_recv()
+            y_copy(u, 0, 1, other).start()
+            y_copy(u, 1, 1, other).start()
+
+        @pl.when(late(u))
+        def _():
+            for way, dy in ((0, -1), (1, 1)):
+                g = genome(dy, 0)
+                y_copy(u, way, 0, g).wait_recv()
+                y_copy(u, way, 2, g, half=True).start()
+                x_copy(u, 1 + way, g).start()
+
+    def relay_again(u):
+        @pl.when(jnp.logical_not(late(u)))
+        def _():
+            behind = genome(-1, 0)
+            y_copy(u, 0, 0, behind).wait_recv()
+            y_copy(u, 0, 2, behind).start()
+            ahead = genome(1, 1)
+            y_copy(u, 1, 1, ahead).wait_recv()
+            y_copy(u, 1, 2, ahead).start()
+
+        @pl.when(late(u))
+        def _():
+            far = genome(2, 0)
+            y_copy(u, 0, 2, far, half=True).wait_recv()
+            y_copy(u, 1, 2, far, half=True).wait_recv()
+            x_copy(u, 3, far).start()
+
+    def settle(u):
+        @pl.when(jnp.logical_not(late(u)))
+        def _():
+            y_copy(u, 0, 1, genome(-1, 1)).wait_recv()
+            y_copy(u, 1, 0, genome(1, 0)).wait_recv()
+            y_copy(u, 0, 2, genome(-2, 0)).wait_recv()
+            y_copy(u, 1, 2, genome(2, 1)).wait_recv()
+
+        @pl.when(late(u))
+        def _():
+            x_copy(u, 0, genome(0, 1)).wait_recv()
+            x_copy(u, 1, genome(-1, 1)).wait_recv()
+            x_copy(u, 2, genome(1, 1)).wait_recv()
+            x_copy(u, 3, genome(2, 1)).wait_recv()
+
+    tile = min(256, acc.shape[1])
+
+    def product(u, at):
+        cols = pl.ds(pl.multiple_of(chip_at(u, -1) * 2 * BLK, 2 * BLK), 2 * BLK)
+        return acc[:, at] + lax.dot_general(
+            gath[u].reshape(WT * BLK, 2 * BLK),
+            wout[at, cols],
+            (((1,), (1,)), ((), ())),
+            preferred_element_type=F32,
+        )
 
     def project(u):
-        y_copy(u, 0, 1, genome(-1, 1)).wait_recv()
-        y_copy(u, 1, 0, genome(1, 0)).wait_recv()
-        y_copy(u, 0, 2, genome(-2, 0)).wait_recv()
-        y_copy(u, 1, 2, genome(2, 1)).wait_recv()
-        owner = (chip - u + nchip) % nchip
-        cols = pl.ds(pl.multiple_of(owner * 2 * BLK, 2 * BLK), 2 * BLK)
-        held = gath[u].reshape(WT * BLK, 2 * BLK)
-        tile = min(256, acc.shape[1])
+        settle(u)
+
+        @pl.when(u == 0)
+        def _():
+            load_wout.wait()
 
         @pl.loop(0, acc.shape[1] // tile)
         def _(n):
             at = pl.ds(pl.multiple_of(n * tile, tile), tile)
-            acc[:, at] += lax.dot_general(
-                held, wout[at, cols], (((1,), (1,)), ((), ())), preferred_element_type=F32
+            acc[:, at] = product(u, at)
+
+    def embed():
+        @pl.loop(1, WT)
+        def _(d):
+            whence = (wt - d + WT) % WT
+            remote(
+                tok_ref, tok_wt.at[whence], tw_send.at[d], tw_recv.at[d], wt_peer(d)
+            ).wait_recv()
+
+        @pl.loop(0, WT // 2)
+        def _(g):
+            hot = jnp.concatenate([one_hot(tok_wt[2 * g]), one_hot(tok_wt[2 * g + 1])], axis=0)
+            acc[pl.ds(pl.multiple_of(g * 2 * BLK, 2 * BLK), 2 * BLK), :] = jnp.dot(
+                hot, emb_ref[...], preferred_element_type=F32
             )
 
-    @pl.loop(-1, nchip + 4)
+    stages = ((0, spread), (2, relay), (4, relay_again), (6, project))
+
+    @pl.loop(0, nchip + stages[-1][0] - 1)
     def _(t):
-        @pl.when(t < nchip)
-        def _():
-            mixer(t)
-
-        for lag, stage in ((1, spread), (2, spread_partner), (3, relay), (4, project)):
+        @pl.when(t < nchip // 2)
+        def _():
+            pl.loop(2 * t, 2 * t + 2)(mixer)
+
+        for lag, stage in stages:
 
             @pl.when((t >= lag) & (t < nchip + lag))
             def _():
                 stage(t - lag)
 
-    @pl.loop(0, WT)
-    def _(g):
-        out_ref[g] = acc[pl.ds(pl.multiple_of(g * BLK, BLK), BLK), :].astype(BF16)
+        pl.when(t == 2)(embed)
+
+    last = nchip - 1
+    settle(last)
+
+    @pl.loop(0, acc.shape[1] // tile)
+    def _(n):
+        at = pl.ds(pl.multiple_of(n * tile, tile), tile)
+        out_ref[:, :, at] = product(last, at).astype(BF16).reshape(WT, BLK, tile)
 
     @pl.loop(1, WT)
     def _(d):
@@ -400,16 +458,26 @@
             def _():
                 block_send(u, i).wait_send()
 
-        x_copy(u, wt).wait_send()
-        for kind in range(3):
+        x_copy(u, 0, wt).wait_send()
+        for way in range(2):
+            y_copy(u, way, 0, wt).wait_send()
+
+        @pl.when(jnp.logical_not(late(u)))
+        def _():
             for way in range(2):
-                y_copy(u, way, kind, wt).wait_send()
+                y_copy(u, way, 1, wt).wait_send()
+                y_copy(u, way, 2, wt).wait_send()
+
+        @pl.when(late(u))
+        def _():
+            for way in range(2):
+                y_copy(u, way, 2, wt, half=True).wait_send()
+            for kind in range(1, 4):
+                x_copy(u, kind, wt).wait_send()
 
 
 def local(nseq, tokens, embed_table, norm_gain, w_in, short_taps, filters, w_out):
     vocab, feats = embed_table.shape
-    taps = filters.shape[1]
-    base = jnp.pad(filters[:, ::-1].astype(F32), ((0, 0), (1, taps - 1)))
     nchip = nseq // 2
     wide = 3 * BLK
     dma = pltpu.SemaphoreType.DMA
@@ -417,7 +485,7 @@
     return pl.pallas_call(
         functools.partial(block_kernel, nseq, feats * WT),
         out_shape=jax.ShapeDtypeStruct((WT, BLK, feats), BF16),
-        in_specs=[vmem] * 6 + [pl.BlockSpec(memory_space=pl.ANY)],
+        in_specs=[vmem] * 6 + [pl.BlockSpec(memory_space=pltpu.HBM)],
         out_specs=vmem,
         scratch_shapes=[
             pltpu.VMEM(w_out.shape, BF16),
@@ -429,8 +497,7 @@
             pltpu.VMEM((nseq, 1, BLK), jnp.int32),
             pltpu.VMEM((WT, 1, BLK), jnp.int32),
             pltpu.VMEM((BLK // GSZ * BLK, 2 * BLK), BF16),
-            pltpu.VMEM((8 + 2 * BLK, wide), F32),
-            pltpu.VMEM((BLK, BLK), BF16),
+            pltpu.VMEM((HALO + 3 * BLK, wide), F32),
             pltpu.VMEM((nchip, 2, BLK, BLK), BF16),
             pltpu.VMEM((nchip, WT, BLK, 2 * BLK), BF16),
             pltpu.VMEM((WT * BLK, feats), F32),
@@ -448,20 +515,22 @@
             dma((WT,)),
             dma((nchip, 2)),
             dma((nchip, 2)),
-            dma((nchip,)),
-            dma((nchip,)),
+            dma((nchip * 4,)),
+            dma((nchip * 4,)),
             dma((nchip * 6,)),
             dma((nchip * 6,)),
         ],
-        compiler_params=pltpu.CompilerParams(collective_id=0, has_side_effects=True),
+        compiler_params=pltpu.CompilerParams(
+            collective_id=0, has_side_effects=True, vmem_limit_bytes=50 * 2**20
+        ),
         name="hyena_block",
     )(
         tokens,
         embed_table,
-        norm_gain.reshape(1, feats),
-        w_in.reshape(feats, wide),
-        short_taps.astype(F32).reshape(3, wide),
-        base,
+        norm_gain,
+        jnp.transpose(w_in, (1, 0, 2)),
+        short_taps,
+        filters,
         w_out,
     )
 

time: 127 us -> 107 us (0.84)
  Pallas kernels: 116 us -> 100 us
  local copies, waits for them, and re-layouts: 8.27 us -> 6.38 us
  other arithmetic: 1.35 us -> 0 us
    pallas_call x1, Pallas kernels: 116 us -> 100 us  [local(): pl.pallas_call(functools.partial(block_kernel, nseq, feats * WT), out_sha...]
    reshape x2 -> x0, local copies, waits for them, and re-layouts: 2.43 us -> none  [the longest x1 1.28 us: local(): norm_gain.reshape(1, feats)]
    unnamed x3 -> x13, local copies, waits for them, and re-layouts: 5.08 us -> 6.38 us
where the time goes in v2:
time: 107 us
  Pallas kernels  100 us (93%)
  local copies, waits for them, and re-layouts  6.38 us (6%)
    pallas_call x1, Pallas kernels, local(): pl.pallas_call(functools.partial(block_kernel, nseq, feats * WT), out_sha...  100 us
    unnamed x13, local copies, waits for them, and re-layouts  6.38 us

profile of v2, /device:TPU:1, one launch (start us, length us, event | category | flops | bytes accessed | tf_op | source)
XLA Modules:
  0.0 106.5 jit_solution(13925597268397137578)
XLA Ops:
  0.0 0.0 copy-start
  0.0 1.2 %copy-done = bf16[512,1024]{1,0:T(8,128)(2,1)S(1)} copy-done((bf16[512,1024]{1,0:T(8,128)(2,1)S(1)}, bf16[512,1024]{1,0:T(8,128)(2,1)}, u32[]{:S(2)}) %copy-start) | copy-done | bytes 1048600
  1.2 0.0 copy-start.1
  1.2 1.1 %copy-done.1 = bf16[1024,3,128]{2,0,1:T(8,128)(2,1)S(1)} copy-done((bf16[1024,3,128]{2,0,1:T(8,128)(2,1)S(1)}, bf16[1024,3,128]{2,0,1:T(8,128)(2,1)}, u32[]{:S(2)}) %copy-start.1) | copy-done | bytes 786456
  2.4 0.0 copy-start.2
  2.4 0.7 copy-done.2
  3.0 0.0 copy-start.3
  3.0 0.7 copy-done.3
  3.7 0.0 copy-start.4
  3.7 0.7 copy-done.4
  4.4 0.0 copy-start.5
  4.4 0.7 copy-done.5
  5.1 100.1 %hyena_block.1 = bf16[8,128,1024]{2,1,0:T(8,128)(2,1)S(1)} custom-call(s32[1,128]{1,0:T(1,128)S(1)} %copy-done.5, bf16[512,1024]{1,0:T(8,128)(2,1)S(1)} %copy-done, bf16[1024]{0:T(1024)(128)(2,1)S(1)} %copy-done.3, bf16[3,1024,128]{2,1,0:T(8,128)(2,1)S(1)} %bitcast.1, bf16[3,3,128]{2,1,0:T(4,128)(2,1)S(1)} %copy-done.2, bf16[8,128]{1,0:T(8,128)(2,1)S(1)} %copy-done.4, ...), custom_call_target="tpu_custom_call" | custom-call | tf_op jit(solution)/shard_map/hyena_block/pallas_call | solution.py:485
  105.2 1.3 %copy.9 = bf16[8,128,1024]{2,1,0:T(8,128)(2,1)} copy(bf16[8,128,1024]{2,1,0:T(8,128)(2,1)S(1)} %hyena_block.1) | data formatting | bytes 4194304
Async XLA Ops:
  0.0 1.2 %copy-start = (bf16[512,1024]{1,0:T(8,128)(2,1)S(1)}, bf16[512,1024]{1,0:T(8,128)(2,1)}, u32[]{:S(2)}) copy-start(bf16[512,1024]{1,0:T(8,128)(2,1)} %emb_ref.1) | copy-start | bytes 3145732
  1.2 1.1 %copy-start.1 = (bf16[1024,3,128]{2,0,1:T(8,128)(2,1)S(1)}, bf16[1024,3,128]{2,0,1:T(8,128)(2,1)}, u32[]{:S(2)}) copy-start(bf16[1024,3,128]{2,0,1:T(8,128)(2,1)} %param.10) | copy-start | bytes 2359300
  2.4 0.7 copy-start.2
  3.0 0.7 copy-start.3
  3.7 0.7 copy-start.4
  4.4 0.7 copy-start.5

commit v3 on v2

--- a/solution.py
+++ b/solution.py
@@ -101,6 +101,13 @@
             barrier, inc=1, device_id=wt_peer(d), device_id_type=pl.DeviceIdType.MESH
         )
 
+    @pl.loop(0, nseq // 2)
+    def _(k):
+        across = {"seq": (1 - chip // nz) * (nseq // 2) + k, "wt": genome(0, 1)}
+        pl.semaphore_signal(
+            barrier, inc=1, device_id=across, device_id_type=pl.DeviceIdType.MESH
+        )
+
     load_wout = pltpu.make_async_copy(wout_hbm, wout, wout_sem)
     load_wout.start()
 
@@ -131,7 +138,7 @@
     tok_seq[seq] = tok_ref[...]
     tok_wt[wt] = tok_ref[...]
 
-    pl.semaphore_wait(barrier, nseq - 1 + WT - 1)
+    pl.semaphore_wait(barrier, nseq - 1 + WT - 1 + nseq // 2)
 
     def part_copy(d):
         return remote(
@@ -200,6 +207,20 @@
             axis=1,
         )
 
+    @pl.loop(1, WT)
+    def _(d):
+        whence = (wt - d + WT) % WT
+        remote(
+            tok_ref, tok_wt.at[whence], tw_send.at[d], tw_recv.at[d], wt_peer(d)
+        ).wait_recv()
+
+    @pl.loop(0, WT // 2)
+    def _(g):
+        hot = jnp.concatenate([one_hot(tok_wt[2 * g]), one_hot(tok_wt[2 * g + 1])], axis=0)
+        acc[pl.ds(pl.multiple_of(g * 2 * BLK, 2 * BLK), 2 * BLK), :] = jnp.dot(
+            hot, emb_ref[...], preferred_element_type=F32
+        )
+
     @pl.loop(1, nseq)
     def _(d):
         whence = (seq - d + nseq) % nseq
@@ -211,22 +232,59 @@
     def _(d):
         vocab_arrival(d).wait_recv()
 
-    steps = [0, 2, -2, 3, -3, 4, 1, -1] if nz == 8 else list(range(nz))
+    def pick(u, values):
+        return sum((jnp.where(u == k, v, 0) for k, v in enumerate(values) if v), 0)
+
+    steps = [0, 1, -1, 2, -2, 3, -3, 4] if nz == 8 else list(range(nz))
+    order = [(flip, step) for step in steps for flip in range(2)]
+    flips = [flip for flip, _ in order]
 
     def offset(u):
-        step = sum(jnp.where(u // 2 == k, v, 0) for k, v in enumerate(steps) if v != 0)
-        return u % 2, step
+        return pick(u, flips), pick(u, [step for _, step in order])
+
+    def direct(u):
+        return pick(u, flips) == 1
+
+    def late(u):
+        return (pick(u, flips) == 0) & (u > 0)
+
+    def crossing(u):
+        return u == 0
 
     def chip_at(u, sign):
         flip, step = offset(u)
         xl, z = chip // nz, chip % nz
         return ((xl + flip) % 2) * nz + (z + sign * step + nz) % nz
 
+    def pick(u, values):
+        return sum((jnp.where(u == k, v, 0) for k, v in enumerate(values) if v), 0)
+
+    steps = [0, 1, -1, 2, -2, 3, -3, 4] if nz == 8 else list(range(nz))
+    order = [(flip, step) for step in steps for flip in range(2)]
+    flips = [flip for flip, _ in order]
+
+    def offset(u):
+        return pick(u, flips), pick(u, [step for _, step in order])
+
+    def direct(u):
+        return pick(u, flips) == 1
+
+    def late(u):
+        return (pick(u, flips) == 0) & (u > 0)
+
+    def crossing(u):
+        return u == 0
+
+    def chip_at(u, sign):
+        flip, step = offset(u)
+        xl, z = chip // nz, chip % nz
+        return ((xl + flip) % 2) * nz + (z + sign * step + nz) % nz
+
     def block_send(u, i):
         to = 2 * chip_at(u, 1) + i
         return remote(
             sbuf.at[u, i],
-            gath.at[u, wt, :, pl.ds(pl.multiple_of(core * BLK, BLK), BLK)],
+            gath.at[u, wt, core],
             s1.at[u, i],
             r1.at[u, core],
             {"seq": to},
@@ -235,17 +293,42 @@
     def block_local(i):
         return pltpu.make_async_copy(
             sbuf.at[0, i],
-            gath.at[0, wt, :, pl.ds(pl.multiple_of(core * BLK, BLK), BLK)],
+            gath.at[0, wt, core],
             self_sem,
         )
 
     def block_arrival(u, i):
         return remote(
             sbuf.at[u, i],
-            gath.at[u, wt, :, pl.ds(i * BLK, BLK)],
+            gath.at[u, wt, i],
             s1.at[u, i],
             r1.at[u, i],
             {"seq": 2 * chip_at(u, 1) + i},
+        )
+
+    def block_send(u, i, twin=0):
+        return remote(
+            sbuf.at[u, i],
+            gath.at[u, wt, core],
+            s1.at[u, 2 * twin + i],
+            r1.at[u, 2 * twin + core],
+            {"seq": 2 * chip_at(u, 1) + i, "wt": genome(0, twin)},
+        )
+
+    def block_local(i):
+        return pltpu.make_async_copy(
+            sbuf.at[0, i],
+            gath.at[0, wt, core],
+            self_sem,
+        )
+
+    def block_arrival(u, i, twin=0):
+        return remote(
+            sbuf.at[u, i],
+            gath.at[u, genome(0, twin), i],
+            s1.at[u, 2 * twin + i],
+            r1.at[u, 2 * twin + i],
+            {"seq": 2 * chip_at(u, 1) + i, "wt": genome(0, twin)},
         )
 
     def mixer(u):
@@ -296,6 +379,10 @@
             def _():
                 block_send(u, i).start()
 
+            @pl.when(direct(u))
+            def _():
+                block_send(u, i, 1).start()
+
     def x_copy(u, kind, g):
         k = u * 4 + kind
         return remote(
@@ -307,11 +394,8 @@
         to = genome(1 if way == 0 else -1, 0)
         part = gath.at[u, g]
         if half:
-            part = gath.at[u, g, way * (BLK // 2) : (way + 1) * (BLK // 2)]
+            part = gath.at[u, g, way]
         return remote(part, part, sy.at[k], ry.at[k], {"wt": to})
-
-    def late(u):
-        return u % 3 == 1
 
     def spread(u):
         for i in range(2):
@@ -327,10 +411,21 @@
 
         y_copy(u, 0, 0, wt).start()
         y_copy(u, 1, 0, wt).start()
-        x_copy(u, 0, wt).start()
+
+        @pl.when(jnp.logical_not(direct(u)))
+        def _():
+            x_copy(u, 0, wt).start()
+
+        @pl.when(direct(u))
+        def _():
+            other = genome(0, 1)
+            for i in range(2):
+                block_arrival(u, i, 1).wait_recv()
+            y_copy(u, 0, 1, other).start()
+            y_copy(u, 1, 1, other).start()
 
     def relay(u):
-        @pl.when(jnp.logical_not(late(u)))
+        @pl.when(crossing(u))
         def _():
             other = genome(0, 1)
             x_copy(u, 0, other).wait_recv()
@@ -382,7 +477,9 @@
     def product(u, at):
         cols = pl.ds(pl.multiple_of(chip_at(u, -1) * 2 * BLK, 2 * BLK), 2 * BLK)
         return acc[:, at] + lax.dot_general(
-            gath[u].reshape(WT * BLK, 2 * BLK),
+            jnp.concatenate(
+                [gath[u, :, i].reshape(WT * BLK, BLK) for i in range(2)], axis=1
+            ),
             wout[at, cols],
             (((1,), (1,)), ((), ())),
             preferred_element_type=F32,
@@ -400,36 +497,20 @@
             at = pl.ds(pl.multiple_of(n * tile, tile), tile)
             acc[:, at] = product(u, at)
 
-    def embed():
-        @pl.loop(1, WT)
-        def _(d):
-            whence = (wt - d + WT) % WT
-            remote(
-                tok_ref, tok_wt.at[whence], tw_send.at[d], tw_recv.at[d], wt_peer(d)
-            ).wait_recv()
-
-        @pl.loop(0, WT // 2)
-        def _(g):
-            hot = jnp.concatenate([one_hot(tok_wt[2 * g]), one_hot(tok_wt[2 * g + 1])], axis=0)
-            acc[pl.ds(pl.multiple_of(g * 2 * BLK, 2 * BLK), 2 * BLK), :] = jnp.dot(
-                hot, emb_ref[...], preferred_element_type=F32
-            )
-
     stages = ((0, spread), (2, relay), (4, relay_again), (6, project))
 
     @pl.loop(0, nchip + stages[-1][0] - 1)
     def _(t):
-        @pl.when(t < nchip // 2)
-        def _():
-            pl.loop(2 * t, 2 * t + 2)(mixer)
+        def mixed(t):
+            return jnp.minimum(jnp.minimum(2 * t + 2, t + 5), nchip)
+
+        pl.loop(mixed(t - 1), mixed(t))(mixer)
 
         for lag, stage in stages:
 
             @pl.when((t >= lag) & (t < nchip + lag))
             def _():
                 stage(t - lag)
-
-        pl.when(t == 2)(embed)
 
     last = nchip - 1
     settle(last)
@@ -458,7 +539,14 @@
             def _():
                 block_send(u, i).wait_send()
 
-        x_copy(u, 0, wt).wait_send()
+            @pl.when(direct(u))
+            def _():
+                block_send(u, i, 1).wait_send()
+
+        @pl.when(jnp.logical_not(direct(u)))
+        def _():
+            x_copy(u, 0, wt).wait_send()
+
         for way in range(2):
             y_copy(u, way, 0, wt).wait_send()
 
@@ -499,7 +587,7 @@
             pltpu.VMEM((BLK // GSZ * BLK, 2 * BLK), BF16),
             pltpu.VMEM((HALO + 3 * BLK, wide), F32),
             pltpu.VMEM((nchip, 2, BLK, BLK), BF16),
-            pltpu.VMEM((nchip, WT, BLK, 2 * BLK), BF16),
+            pltpu.VMEM((nchip, WT, 2, BLK, BLK), BF16),
             pltpu.VMEM((WT * BLK, feats), F32),
             dma,
             dma,
@@ -513,8 +601,8 @@
             dma((nseq,)),
             dma((WT,)),
             dma((WT,)),
-            dma((nchip, 2)),
-            dma((nchip, 2)),
+            dma((nchip, 4)),
+            dma((nchip, 4)),
             dma((nchip * 4,)),
             dma((nchip * 4,)),
             dma((nchip * 6,)),
@@ -525,13 +613,18 @@
         ),
         name="hyena_block",
     )(
-        tokens,
-        embed_table,
-        norm_gain,
-        jnp.transpose(w_in, (1, 0, 2)),
-        short_taps,
-        filters,
-        w_out,
+        *(
+            pltpu.with_memory_space_constraint(x, pltpu.HBM)
+            for x in (
+                tokens,
+                embed_table,
+                norm_gain,
+                jnp.transpose(w_in, (1, 0, 2)),
+                short_taps,
+                filters,
+                w_out,
+            )
+        )
     )
 
 

time: 107 us -> 102 us (0.953); the launches traced: 107 us -> 100 us
  local copies, waits for them, and re-layouts: 6.38 us -> 1.32 us
    unnamed x13 -> x1, local copies, waits for them, and re-layouts: 6.38 us -> 1.32 us
where the time goes in v3:
time: 102 us; the launch traced here: 100 us
  Pallas kernels  99.1 us (97%)
  local copies, waits for them, and re-layouts  1.32 us (1%)
    pallas_call x1, Pallas kernels, local(): pl.pallas_call(functools.partial(block_kernel, nseq, feats * WT), out_sha...  99.1 us

profile of v3, /device:TPU:1, one launch (start us, length us, event | category | flops | bytes accessed | tf_op | source)
XLA Modules:
  0.0 100.5 jit_solution(13059195945228156424)
XLA Ops:
  0.0 99.1 %hyena_block.1 = bf16[8,128,1024]{2,1,0:T(8,128)(2,1)S(1)} custom-call(s32[1,128]{1,0:T(1,128)} %tok_ref.1, bf16[512,1024]{1,0:T(8,128)(2,1)} %emb_ref.1, bf16[1024]{0:T(1024)(128)(2,1)} %gain_ref.1, bf16[3,1024,128]{2,1,0:T(8,128)(2,1)} %bitcast.1, bf16[3,3,128]{2,1,0:T(4,128)(2,1)} %taps_ref.1, bf16[8,128]{1,0:T(8,128)(2,1)} %filt_ref.1, ...), custom_call_target="tpu_custom_call" | custom-call | tf_op jit(solution)/shard_map/hyena_block/pallas_call | solution.py:573
  99.1 1.3 %copy.9 = bf16[8,128,1024]{2,1,0:T(8,128)(2,1)} copy(bf16[8,128,1024]{2,1,0:T(8,128)(2,1)S(1)} %hyena_block.1) | data formatting | bytes 4194304

commit v4 on v3

--- a/solution.py
+++ b/solution.py
@@ -66,6 +66,7 @@
     y, xh = wt // 2, wt % 2
     vocab = emb_ref.shape[0]
     vrow = vocab // WT
+    half = vrow // 2
     wide = 3 * BLK
 
     def genome(dy, flip):
@@ -125,7 +126,7 @@
         streams = jnp.concatenate([win_ref[k] for k in range(3)], axis=1)
         p = jnp.dot(gained, streams, preferred_element_type=F32).astype(BF16)
         for k in range(WT // 2):
-            part_out[i * (WT // 2) + k] = p[k * vrow : (k + 1) * vrow]
+            part_out[i * (WT // 2) + k] = p[k * vrow : (k + 1) * vrow].reshape(2, half, wide)
 
     filt = filt_ref[...].astype(F32)
     for q in range(BLK // GSZ):
@@ -140,9 +141,13 @@
 
     pl.semaphore_wait(barrier, nseq - 1 + WT - 1 + nseq // 2)
 
-    def part_copy(d):
-        return remote(
-            part_out.at[(wt + d) % WT], part_in.at[d], p_send.at[d], p_recv.at[d], wt_peer(d)
+    def part_copy(d, h):
+        return remote(
+            part_out.at[(wt + d) % WT, h],
+            part_in.at[d, h],
+            p_send.at[h, d],
+            p_recv.at[h, d],
+            wt_peer(d),
         )
 
     def sq_copy(d):
@@ -157,7 +162,11 @@
     @pl.loop(1, WT)
     def _(d):
         sq_copy(d).start()
-        part_copy(d).start()
+        part_copy(d, 0).start()
+
+    @pl.loop(1, WT)
+    def _(d):
+        part_copy(d, 1).start()
 
     @pl.loop(1, WT)
     def _(d):
@@ -167,34 +176,42 @@
     def _(d):
         tok_seq_copy(d).start()
 
+    def vocab_copy(d, h):
+        return remote(
+            vtab.at[wt, h], vtab.at[wt, h], v_send.at[h, d], v_recv.at[h, d], wt_peer(d)
+        )
+
+    def vocab_arrival(d, h):
+        whence = (wt - d + WT) % WT
+        return remote(
+            vtab.at[whence, h], vtab.at[whence, h], v_send.at[h, d], v_recv.at[h, d], wt_peer(d)
+        )
+
     @pl.loop(1, WT)
     def _(d):
         sq_copy(d).wait_recv()
-        part_copy(d).wait_recv()
-
-    total = part_out[wt].astype(F32)
+
     squares = sq_out[...]
     for d in range(1, WT):
-        total = total + part_in[d].astype(F32)
         squares = squares + sq_in[d]
     scale = lax.rsqrt(squares / feature_count + 1e-06)
-    r = lax.broadcasted_iota(jnp.int32, (vrow, vocab), 0) + wt * vrow
-    l = lax.broadcasted_iota(jnp.int32, (vrow, vocab), 1)
-    scale_col = jnp.sum(jnp.where(r == l, scale, 0.0), axis=1, keepdims=True)
-    vtab[wt] = (total * scale_col).astype(BF16)
-
-    def vocab_copy(d):
-        return remote(vtab.at[wt], vtab.at[wt], v_send.at[d], v_recv.at[d], wt_peer(d))
-
-    def vocab_arrival(d):
-        whence = (wt - d + WT) % WT
-        return remote(
-            vtab.at[whence], vtab.at[whence], v_send.at[d], v_recv.at[d], wt_peer(d)
-        )
-
-    @pl.loop(1, WT)
-    def _(d):
-        vocab_copy(d).start()
+    for h in range(2):
+
+        @pl.loop(1, WT)
+        def _(d):
+            part_copy(d, h).wait_recv()
+
+        total = part_out[wt, h].astype(F32)
+        for d in range(1, WT):
+            total = total + part_in[d, h].astype(F32)
+        r = lax.broadcasted_iota(jnp.int32, (half, vocab), 0) + wt * vrow + h * half
+        l = lax.broadcasted_iota(jnp.int32, (half, vocab), 1)
+        scale_col = jnp.sum(jnp.where(r == l, scale, 0.0), axis=1, keepdims=True)
+        vtab[wt, h] = (total * scale_col).astype(BF16)
+
+        @pl.loop(1, WT)
+        def _(d):
+            vocab_copy(d, h).start()
 
     def one_hot(row):
         cols = jnp.broadcast_to(row, (BLK, BLK)).T
@@ -230,7 +247,8 @@
 
     @pl.loop(1, WT)
     def _(d):
-        vocab_arrival(d).wait_recv()
+        for h in range(2):
+            vocab_arrival(d, h).wait_recv()
 
     def pick(u, values):
         return sum((jnp.where(u == k, v, 0) for k, v in enumerate(values) if v), 0)
@@ -474,30 +492,40 @@
 
     tile = min(256, acc.shape[1])
 
-    def product(u, at):
-        cols = pl.ds(pl.multiple_of(chip_at(u, -1) * 2 * BLK, 2 * BLK), 2 * BLK)
+    def product(units, at):
+        held = [gath[u, :, i].reshape(WT * BLK, BLK) for u in units for i in range(2)]
+        weights = [
+            wout[at, pl.ds(pl.multiple_of(chip_at(u, -1) * 2 * BLK, 2 * BLK), 2 * BLK)]
+            for u in units
+        ]
         return acc[:, at] + lax.dot_general(
-            jnp.concatenate(
-                [gath[u, :, i].reshape(WT * BLK, BLK) for i in range(2)], axis=1
-            ),
-            wout[at, cols],
+            jnp.concatenate(held, axis=1),
+            jnp.concatenate(weights, axis=1),
             (((1,), (1,)), ((), ())),
             preferred_element_type=F32,
         )
 
-    def project(u):
-        settle(u)
-
-        @pl.when(u == 0)
-        def _():
-            load_wout.wait()
+    def project(units):
+        for u in units:
+            settle(u)
 
         @pl.loop(0, acc.shape[1] // tile)
         def _(n):
             at = pl.ds(pl.multiple_of(n * tile, tile), tile)
-            acc[:, at] = product(u, at)
-
-    stages = ((0, spread), (2, relay), (4, relay_again), (6, project))
+            acc[:, at] = product(units, at)
+
+    def project_some(u):
+        pl.when(u == 0)(load_wout.wait)
+
+        @pl.when((u % 2 == 1) & (u < nchip - 1))
+        def _():
+            project((u - 1, u))
+
+        @pl.when(u == nchip - 2)
+        def _():
+            project((u,))
+
+    stages = ((0, spread), (2, relay), (4, relay_again), (8, project_some))
 
     @pl.loop(0, nchip + stages[-1][0] - 1)
     def _(t):
@@ -518,14 +546,15 @@
     @pl.loop(0, acc.shape[1] // tile)
     def _(n):
         at = pl.ds(pl.multiple_of(n * tile, tile), tile)
-        out_ref[:, :, at] = product(last, at).astype(BF16).reshape(WT, BLK, tile)
+        out_ref[:, :, at] = product((last,), at).astype(BF16).reshape(WT, BLK, tile)
 
     @pl.loop(1, WT)
     def _(d):
         sq_copy(d).wait_send()
-        part_copy(d).wait_send()
+        for h in range(2):
+            part_copy(d, h).wait_send()
+            vocab_copy(d, h).wait_send()
         tok_wt_copy(d).wait_send()
-        vocab_copy(d).wait_send()
 
     @pl.loop(1, nseq)
     def _(d):
@@ -577,11 +606,11 @@
         out_specs=vmem,
         scratch_shapes=[
             pltpu.VMEM(w_out.shape, BF16),
-            pltpu.VMEM((WT, vocab // WT, wide), BF16),
-            pltpu.VMEM((WT, vocab // WT, wide), BF16),
+            pltpu.VMEM((WT, 2, vocab // WT // 2, wide), BF16),
+            pltpu.VMEM((WT, 2, vocab // WT // 2, wide), BF16),
             pltpu.VMEM((1, vocab), F32),
             pltpu.VMEM((WT, 1, vocab), F32),
-            pltpu.VMEM((WT, vocab // WT, wide), BF16),
+            pltpu.VMEM((WT, 2, vocab // WT // 2, wide), BF16),
             pltpu.VMEM((nseq, 1, BLK), jnp.int32),
             pltpu.VMEM((WT, 1, BLK), jnp.int32),
             pltpu.VMEM((BLK // GSZ * BLK, 2 * BLK), BF16),
@@ -591,12 +620,12 @@
             pltpu.VMEM((WT * BLK, feats), F32),
             dma,
             dma,
+            dma((2, WT)),
+            dma((2, WT)),
             dma((WT,)),
             dma((WT,)),
-            dma((WT,)),
-            dma((WT,)),
-            dma((WT,)),
-            dma((WT,)),
+            dma((2, WT)),
+            dma((2, WT)),
             dma((nseq,)),
             dma((nseq,)),
             dma((WT,)),

time: 102 us -> 98.4 us (0.965); the launches traced: 100 us -> 98.3 us
  Pallas kernels: 99.1 us -> 97 us
    pallas_call x1, Pallas kernels: 99.1 us -> 97 us  [local(): pl.pallas_call(functools.partial(block_kernel, nseq, feats * WT), out_sha...]
where the time goes in v4:
time: 98.4 us; the launch traced here: 98.3 us
  Pallas kernels  97 us (99%)
  local copies, waits for them, and re-layouts  1.32 us (1%)
    pallas_call x1, Pallas kernels, local(): pl.pallas_call(functools.partial(block_kernel, nseq, feats * WT), out_sha...  97 us

profile of v4, /device:TPU:1, one launch (start us, length us, event | category | flops | bytes accessed | tf_op | source)
XLA Modules:
  0.0 98.3 jit_solution(4446499470840996665)
XLA Ops:
  0.0 97.0 %hyena_block.1 = bf16[8,128,1024]{2,1,0:T(8,128)(2,1)S(1)} custom-call(s32[1,128]{1,0:T(1,128)} %tok_ref.1, bf16[512,1024]{1,0:T(8,128)(2,1)} %emb_ref.1, bf16[1024]{0:T(1024)(128)(2,1)} %gain_ref.1, bf16[3,1024,128]{2,1,0:T(8,128)(2,1)} %bitcast.1, bf16[3,3,128]{2,1,0:T(4,128)(2,1)} %taps_ref.1, bf16[8,128]{1,0:T(8,128)(2,1)} %filt_ref.1, ...), custom_call_target="tpu_custom_call" | custom-call | tf_op jit(solution)/shard_map/hyena_block/pallas_call | solution.py:602
  97.0 1.3 %copy.9 = bf16[8,128,1024]{2,1,0:T(8,128)(2,1)} copy(bf16[8,128,1024]{2,1,0:T(8,128)(2,1)S(1)} %hyena_block.1) | data formatting | bytes 4194304
